TPU v7x, 32 devices: a whole 2x2x4 slice. The times are simulated.
32 devices in a mesh: dp: 8 (over z, y), tensor: 4 (over x, core).
Axes of the slice: x: 2, y: 2, z: 4, core: 2. Of those that a mesh axis runs over, the one named last changes fastest.
Arguments:
- tokens: bfloat16 [3, 4096, 1536], P(None, ('dp', 'tensor')), may hold values from -6 to 6
- lengths: int32 [3, 32, 6], P(None, ('dp', 'tensor')), may hold values from 1 to 64, 128 in all within a row
- first_gain: bfloat16 [1536], P(('dp', 'tensor')), may hold values from 0.099609375 to 1.8984375
- query_weight: bfloat16 [1536, 1536], P(('dp', 'tensor')), may hold values from -0.15625 to 0.15625
- key_weight: bfloat16 [1536, 768], P(('dp', 'tensor')), may hold values from -0.15625 to 0.15625
- value_weight: bfloat16 [1536, 768], P(('dp', 'tensor')), may hold values from -0.15625 to 0.15625
- output_weight: bfloat16 [1536, 1536], P(('dp', 'tensor')), may hold values from -0.4375 to 0.4375
- second_gain: bfloat16 [1536], P(('dp', 'tensor')), may hold values from 0.099609375 to 1.8984375
- gate_weight: bfloat16 [1536, 4096], P('dp', 'tensor'), may hold values from -0.15625 to 0.15625
- up_weight: bfloat16 [1536, 4096], P('dp', 'tensor'), may hold values from -0.15625 to 0.15625
- down_weight: bfloat16 [4096, 1536], P('tensor', 'dp'), may hold values from -0.09375 to 0.09375
- cotangent: bfloat16 [3, 4096, 1536], P(None, ('dp', 'tensor')), may hold values from -6 to 6
Outputs:
- layer_out: bfloat16 [3, 4096, 1536], P(None, ('dp', 'tensor'))
- input_grad: float32 [3, 4096, 1536], P(None, ('dp', 'tensor'))
- first_gain_grad: float32 [1536], P(('dp', 'tensor'))
- query_grad: float32 [1536, 1536], P(('dp', 'tensor'))
- key_grad: float32 [1536, 768], P(('dp', 'tensor'))
- value_grad: float32 [1536, 768], P(('dp', 'tensor'))
- output_grad: float32 [1536, 1536], P(('dp', 'tensor'))
- second_gain_grad: float32 [1536], P(('dp', 'tensor'))
- gate_grad: float32 [1536, 4096], P('dp', 'tensor')
- up_grad: float32 [1536, 4096], P('dp', 'tensor')
- down_grad: float32 [4096, 1536], P('tensor', 'dp')
Inputs may be any that keep to these rules, and one draw needn't show every extreme that they name: Row lengths[m, p] splits the 128 rows of pack p of micro-batch m into 6 runs in order, summing to 128; the first 5 runs are sequences, the last is padding; no run is longer than 64 rows.
All inputs are finite; a program needn't handle non-finite values.
Results may differ from a plain program's by a relative error of at most 0.013.
Values may be sent and summed in bfloat16 or wider, within the bound.
No kernel may reach another device: no remote copies, remote signals or barrier semaphores. Data moves between devices by JAX's collectives and lax.ppermute only.
A program may use at most 192 MiB of HBM per device.

v0:
```python
import math
import jax
import jax.numpy as jnp
from jax import lax
from jax.sharding import PartitionSpec as P

HEADS = 16
KV_HEADS = 8
HEAD = 96
SLOTS = 6
GROUP = HEADS // KV_HEADS
LANES = 128
EPSILON = 1e-05
ROPE_BASE = 100000.0
NEG_LARGE = -1e30
AXES = ("dp", "tensor")
bf16 = jnp.bfloat16
f32 = jnp.float32


def pack_layout(seq_lengths, row_count):
    seq_ends = jnp.cumsum(seq_lengths)
    seq_starts = seq_ends - seq_lengths
    row_index = jnp.arange(row_count, dtype=jnp.int32)
    segment = jnp.sum((row_index[:, None] >= seq_ends[None, :]).astype(jnp.int32), axis=1)
    owner_hot = segment[:, None] == jnp.arange(seq_lengths.shape[0], dtype=jnp.int32)[None, :]
    position = row_index - jnp.sum(jnp.where(owner_hot, seq_starts[None, :], 0), axis=1)
    return (segment, position)


def rotary_tables(position, head_size):
    half_size = head_size // 2
    freq_index = jnp.arange(half_size, dtype=f32)
    inverse = jnp.exp(freq_index * (-2.0 / head_size) * math.log(ROPE_BASE))
    angles = position.astype(f32)[..., None] * inverse
    return (jnp.cos(angles), jnp.sin(angles))


def rotate(vectors, cosine, sine_part):
    half_size = vectors.shape[-1] // 2
    lower_half = vectors[..., :half_size]
    upper_half = vectors[..., half_size:]
    cosine = cosine[..., None, :]
    sine_part = sine_part[..., None, :]
    return jnp.concatenate(
        [
            lower_half * cosine - upper_half * sine_part,
            upper_half * cosine + lower_half * sine_part,
        ],
        axis=-1,
    )


def product(left_side, right_side):
    return jnp.dot(left_side, right_side, preferred_element_type=f32)


def across(left_side, right_side):
    return lax.dot_general(
        left_side, right_side, (((0,), (0,)), ((), ())), preferred_element_type=f32
    )


def against(left_side, right_side):
    return lax.dot_general(
        left_side, right_side, (((1,), (1,)), ((), ())), preferred_element_type=f32
    )


def bits_of(size):
    return [1 << k for k in range(size.bit_length() - 1)]


def near_first(size):
    masks = bits_of(size)
    return masks[:1] + masks[:0:-1]


def far_first(size):
    return bits_of(size)[::-1]


def rel_source(me, masks, block, count):
    place = jnp.arange(count, dtype=jnp.int32)
    step = place // block
    delta = jnp.zeros_like(step)
    for k, mask in enumerate(masks):
        delta = delta + (step >> k & 1) * mask
    return (me ^ delta) * block + place % block


def one_hot(source):
    count = source.shape[0]
    rows = lax.broadcasted_iota(jnp.int32, (count, count), 0)
    return (rows == source[None, :]).astype(bf16)


def join(parts):
    return parts[0] if len(parts) == 1 else jnp.concatenate(parts, axis=0)


def program(sizes):
    dp_n, tp_n = (sizes["dp"], sizes["tensor"])
    world = dp_n * tp_n

    def swap(array, mask):
        return lax.ppermute(array, AXES, [(i, i ^ mask) for i in range(world)])

    def gather(own, masks, loose):
        held = [own]
        for k, mask in enumerate(masks):
            got = [swap(part, mask) for part in held]
            held = held + got
            if k < len(masks) - loose:
                held = [join(held)]
        return held

    def per_device(
        tokens,
        lengths,
        first_gain,
        query_weight,
        key_weight,
        value_weight,
        output_weight,
        second_gain,
        gate_weight,
        up_weight,
        down_weight,
        cotangent,
    ):
        micro, per_pack, width = tokens.shape
        rows = micro * per_pack
        qw, kw = (query_weight.shape[1], key_weight.shape[1])
        ff = gate_weight.shape[1]
        wide = qw + 2 * kw
        shard = query_weight.shape[0]
        dp_i, t_i = (lax.axis_index("dp"), lax.axis_index("tensor"))
        me = dp_i * tp_n + t_i
        dp_attn = [m * tp_n for m in near_first(dp_n)]
        t_bits = bits_of(tp_n)[::-1]
        attn_masks = dp_attn + t_bits
        mlp_masks = [m * tp_n for m in far_first(dp_n)]
        x_low = tokens.reshape(rows, width)
        dy_low = cotangent.reshape(rows, width)
        gains = jnp.pad(jnp.stack([first_gain, second_gain], axis=1), ((0, 0), (0, LANES - 2)))
        own_qkv = jnp.concatenate([query_weight, key_weight, value_weight, gains], axis=1)
        own_gu = jnp.concatenate([gate_weight, up_weight], axis=1)
        own_down = down_weight.T

        def gather_attn(own):
            held = gather(own, dp_attn, 2)
            far = [swap(part, t_bits[0]) for part in held]
            pieces = [join(held), join(far)]
            for mask in t_bits[1:]:
                pieces = pieces + [swap(part, mask) for part in pieces]
            return pieces

        qkv_pieces = gather_attn(own_qkv)
        out_pieces = gather_attn(output_weight)
        gu_full = join(gather(own_gu, mlp_masks, 3))
        down_full = join(gather(own_down, mlp_masks, 3))
        n_pieces = len(qkv_pieces)
        part = width // n_pieces
        pick_attn = one_hot(rel_source(me, attn_masks, shard, width))
        mlp_source = rel_source(dp_i, [m // tp_n for m in mlp_masks], shard * tp_n, width)
        pick_mlp = one_hot(mlp_source)

        def order(array, pick):
            return product(array, pick).astype(bf16)

        def restore(array, pick):
            return against(array, pick)

        gains_rel = jnp.concatenate([piece[:, wide : wide + 2] for piece in qkv_pieces], axis=0)
        g1_rel = gains_rel[:, 0].astype(f32)
        g2 = restore(gains_rel[:, 1][None, :], pick_attn)[0]
        segment, position = jax.vmap(lambda own: pack_layout(own, per_pack))(lengths[:, 0])
        cosine, sine_part = rotary_tables(position, HEAD)
        row_index = jnp.arange(per_pack, dtype=jnp.int32)
        allowed = (
            (segment[:, :, None] == segment[:, None, :])
            & (row_index[None, None, :] <= row_index[None, :, None])
            & (segment < SLOTS - 1)[:, :, None]
        )[:, None, None]
        factor = 1.0 / math.sqrt(HEAD)
        inputs = x_low.astype(f32)
        r1 = lax.rsqrt(jnp.mean(inputs * inputs, axis=1, keepdims=True) + EPSILON)
        x_rel = order(x_low, pick_attn).astype(f32)
        n1_rel = (x_rel * r1 * g1_rel).astype(bf16)
        n1_parts = [n1_rel[:, k * part : (k + 1) * part] for k in range(n_pieces)]
        qkv = sum((product(a, b) for a, b in zip(n1_parts, qkv_pieces)))
        shape = (micro, per_pack)
        queries = rotate(qkv[:, :qw].reshape(shape + (HEADS, HEAD)), cosine, sine_part)
        queries = queries.astype(bf16).reshape(shape + (KV_HEADS, GROUP, HEAD))
        keys = rotate(
            qkv[:, qw : qw + kw].reshape(shape + (KV_HEADS, HEAD)), cosine, sine_part
        ).astype(bf16)
        values = qkv[:, qw + kw : wide].astype(bf16).reshape(shape + (KV_HEADS, HEAD))
        scores = jnp.einsum("pqhgd,pkhd->phgqk", queries, keys, preferred_element_type=f32) * factor
        row_peak = jnp.max(jnp.where(allowed, scores, NEG_LARGE), axis=-1, keepdims=True)
        raised = jnp.where(allowed, jnp.exp(jnp.where(allowed, scores - row_peak, 0.0)), 0.0)
        totals = jnp.sum(raised, axis=-1, keepdims=True)
        probs = raised / jnp.where(totals > 0, totals, 1.0)
        probs_low = probs.astype(bf16)
        attended = jnp.einsum("phgqk,pkhd->pqhgd", probs_low, values, preferred_element_type=f32)
        attended = attended.reshape(rows, qw).astype(bf16)
        att_rel = order(attended, pick_attn)
        att_parts = [att_rel[:, k * part : (k + 1) * part] for k in range(n_pieces)]
        middle = inputs + sum((product(a, b) for a, b in zip(att_parts, out_pieces)))
        r2 = lax.rsqrt(jnp.mean(middle * middle, axis=1, keepdims=True) + EPSILON)
        n2 = (middle * r2 * g2).astype(bf16)
        n2_rel = order(n2, pick_mlp)
        dy_rel = order(dy_low, pick_mlp)

        def spread(own):
            return join(gather(own, t_bits, tp_n))

        def collect(partial):
            for mask in t_bits[::-1]:
                half = partial.shape[0] // 2
                got = swap(partial[half:].astype(bf16), mask)
                partial = partial[:half].astype(f32) + got.astype(f32)
            return partial

        dy_all = spread(dy_rel)
        n2_all = spread(n2_rel)
        gu = product(n2_all, gu_full)
        gate, up = (gu[:, :ff], gu[:, ff:])
        sig = jax.nn.sigmoid(gate)
        hidden = (gate * sig * up).astype(bf16)
        dhid = product(dy_all, down_full)
        dgate = (dhid * up * sig * (1.0 + gate * (1.0 - sig))).astype(bf16)
        dup = (dhid * gate * sig).astype(bf16)
        dgu = jnp.concatenate([dgate, dup], axis=1)
        dn2 = restore(collect(against(dgu, gu_full).astype(bf16)).astype(bf16), pick_mlp)
        down_sum = collect(against(hidden, down_full).astype(bf16)).astype(bf16)
        layer_out = (middle + restore(down_sum, pick_mlp)).astype(bf16)

        def reduce_rows(own_half, sent_half, masks):
            total = own_half() + swap(sent_half().astype(bf16), masks[0]).astype(f32)
            for mask in masks[1:]:
                half = total.shape[0] // 2
                got = swap(total[half:].astype(bf16), mask)
                total = total[:half] + got.astype(f32)
            return total

        half = width // 2

        def mlp_grad(left, right):
            return reduce_rows(
                lambda: across(left[:, :half], right),
                lambda: across(left[:, half:], right),
                mlp_masks[::-1],
            )

        down_grad = mlp_grad(dy_all, hidden).T
        gate_grad = mlp_grad(n2_all, dgate)
        up_grad = mlp_grad(n2_all, dup)
        dy = dy_low.astype(f32)
        weighted = dn2 * g2
        dmid = (
            dy
            + r2 * weighted
            - middle * (r2 * r2 * r2) * jnp.mean(weighted * middle, axis=1, keepdims=True)
        )
        dmb = dmid.astype(bf16)

        def attn_grad(lefts, right):
            held = [across(left, right) for left in lefts]
            for mask in t_bits[1:][::-1]:
                n = len(held) // 2
                got = [swap(piece.astype(bf16), mask) for piece in held[n:]]
                held = [a + b.astype(f32) for a, b in zip(held[:n], got)]
            return reduce_rows(lambda: held[0], lambda: held[1], [t_bits[0]] + dp_attn[::-1])

        output_grad = attn_grad(att_parts, dmb)
        datt_rel = jnp.concatenate([against(dmb, piece) for piece in out_pieces], axis=1)
        datt = restore(datt_rel.astype(bf16), pick_attn).astype(bf16)
        datt = datt.reshape(shape + (KV_HEADS, GROUP, HEAD))
        dprob = jnp.einsum("pqhgd,pkhd->phgqk", datt, values, preferred_element_type=f32)
        delta = jnp.sum(probs * dprob, axis=-1, keepdims=True)
        dscore = (probs * (dprob - delta)).astype(bf16)
        dvalue = jnp.einsum("phgqk,pqhgd->pkhd", probs_low, datt, preferred_element_type=f32)
        dqr = jnp.einsum("phgqk,pkhd->pqhgd", dscore, keys, preferred_element_type=f32) * factor
        dkr = jnp.einsum("phgqk,pqhgd->pkhd", dscore, queries, preferred_element_type=f32) * factor
        dq = rotate(dqr.reshape(shape + (HEADS, HEAD)), cosine, -sine_part)
        dk = rotate(dkr, cosine, -sine_part)
        dqkv = jnp.concatenate(
            [
                dq.astype(bf16).reshape(rows, qw),
                dk.astype(bf16).reshape(rows, kw),
                dvalue.astype(bf16).reshape(rows, kw),
            ],
            axis=1,
        )
        qkv_grad = attn_grad(n1_parts, dqkv)
        dn1_rel = jnp.concatenate([against(dqkv, piece[:, :wide]) for piece in qkv_pieces], axis=1)
        weighted = dn1_rel * g1_rel
        part_rel = r1 * weighted - x_rel * (r1 * r1 * r1) * jnp.mean(
            weighted * x_rel, axis=1, keepdims=True
        )
        high = part_rel.astype(bf16)
        low = (part_rel - high.astype(f32)).astype(bf16)
        input_grad = dmid + restore(high, pick_attn) + restore(low, pick_attn)
        own_wide = own_qkv[:, :wide].astype(f32)
        first_gain_grad = jnp.sum(own_wide * qkv_grad, axis=1) / first_gain.astype(f32)
        second = jnp.sum(
            gate_weight.astype(f32) * gate_grad + up_weight.astype(f32) * up_grad, axis=1
        )
        second = lax.psum(second, "tensor")
        second = lax.dynamic_slice(second, (t_i * shard,), (shard,))
        second_gain_grad = second / second_gain.astype(f32)
        return (
            layer_out.reshape(tokens.shape),
            input_grad.reshape(tokens.shape),
            first_gain_grad,
            qkv_grad[:, :qw],
            qkv_grad[:, qw : qw + kw],
            qkv_grad[:, qw + kw :],
            output_grad,
            second_gain_grad,
            gate_grad,
            up_grad,
            down_grad,
        )

    return per_device


def solution(mesh):
    rows = P(None, AXES, None)
    split = P(AXES, None)
    placed = (
        rows,
        rows,
        P(AXES),
        split,
        split,
        split,
        split,
        P(AXES),
        P("dp", "tensor"),
        P("dp", "tensor"),
        P("tensor", "dp"),
        rows,
    )
    return jax.shard_map(
        program(dict(mesh.shape)),
        mesh=mesh,
        in_specs=placed,
        out_specs=(
            rows,
            rows,
            P(AXES),
            split,
            split,
            split,
            split,
            P(AXES),
            P("dp", "tensor"),
            P("dp", "tensor"),
            P("tensor", "dp"),
        ),
        check_vma=False,
    )
```

profile of v0, /device:TPU:0, one launch (start us, length us, event | category | flops | bytes accessed | tf_op | source)
XLA Modules:
  0.0 805.7 jit_solution(15397457779507763800)
XLA Ops:
  29.8 8.6 %collective-permute-done.4 = bf16[96,3200]{1,0:T(8,128)(2,1)S(1)} collective-permute-done((bf16[96,3200]{1,0:T(8,128)(2,1)S(1)}, bf16[96,3200]{1,0:T(8,128)(2,1)S(1)}, u32[]{:S(2)}, u32[]{:S(2)}) %collective-permute-start.4) | collective-permute-done | bytes 614432 | tf_op jit(solution)/shard_map/ppermute | solution.py:107
  39.7 27.5 %collective-permute-done.1 = bf16[96,3200]{1,0:T(8,128)(2,1)S(1)} collective-permute-done((bf16[96,3200]{1,0:T(8,128)(2,1)S(1)}, bf16[96,3200]{1,0:T(8,128)(2,1)S(1)}, u32[]{:S(2)}, u32[]{:S(2)}) %collective-permute-start.1) | collective-permute-done | bytes 614432 | tf_op jit(solution)/shard_map/ppermute | solution.py:107
  76.1 8.4 %collective-permute-done.3 = bf16[96,3200]{1,0:T(8,128)(2,1)S(1)} collective-permute-done((bf16[96,3200]{1,0:T(8,128)(2,1)S(1)}, bf16[96,3200]{1,0:T(8,128)(2,1)S(1)}, u32[]{:S(2)}, u32[]{:S(2)}) %collective-permute-start.3) | collective-permute-done | bytes 614432 | tf_op jit(solution)/shard_map/ppermute | solution.py:107
  88.3 13.0 %collective-permute-done.6 = bf16[96,3200]{1,0:T(8,128)(2,1)S(1)} collective-permute-done((bf16[96,3200]{1,0:T(8,128)(2,1)S(1)}, bf16[96,3200]{1,0:T(8,128)(2,1)S(1)}, u32[]{:S(2)}, u32[]{:S(2)}) %collective-permute-start.6) | collective-permute-done | bytes 614432 | tf_op jit(solution)/shard_map/ppermute | solution.py:107
  102.2 9.9 %collective-permute-done.7 = bf16[96,3200]{1,0:T(8,128)(2,1)S(1)} collective-permute-done((bf16[96,3200]{1,0:T(8,128)(2,1)S(1)}, bf16[96,3200]{1,0:T(8,128)(2,1)S(1)}, u32[]{:S(2)}, u32[]{:S(2)}) %collective-permute-start.7) | collective-permute-done | bytes 614432 | tf_op jit(solution)/shard_map/ppermute | solution.py:107
  141.3 7.3 collective-permute-done.34
  149.2 23.1 %collective-permute-done.23 = bf16[192,2048]{1,0:T(8,128)(2,1)S(1)} collective-permute-done((bf16[192,2048]{1,0:T(8,128)(2,1)}, bf16[192,2048]{1,0:T(8,128)(2,1)S(1)}, u32[]{:S(2)}, u32[]{:S(2)}) %collective-permute-start.23) | collective-permute-done | bytes 786464 | tf_op jit(solution)/shard_map/ppermute | solution.py:107
  254.1 18.8 %collective-permute-done.36 = bf16[192,1024]{1,0:T(8,128)(2,1)S(1)} collective-permute-done((bf16[192,1024]{1,0:T(8,128)(2,1)S(1)}, bf16[192,1024]{1,0:T(8,128)(2,1)S(1)}, u32[]{:S(2)}, u32[]{:S(2)}) %collective-permute-start.36) | collective-permute-done | bytes 393248 | tf_op jit(solution)/shard_map/ppermute | solution.py:107
  280.2 13.4 %collective-permute-done.28 = bf16[192,2048]{1,0:T(8,128)(2,1)S(1)} collective-permute-done((bf16[192,2048]{1,0:T(8,128)(2,1)}, bf16[192,2048]{1,0:T(8,128)(2,1)S(1)}, u32[]{:S(2)}, u32[]{:S(2)}) %collective-permute-start.28) | collective-permute-done | bytes 786464 | tf_op jit(solution)/shard_map/ppermute | solution.py:107
  295.1 13.2 %collective-permute-done.29 = bf16[192,2048]{1,0:T(8,128)(2,1)S(1)} collective-permute-done((bf16[192,2048]{1,0:T(8,128)(2,1)S(1)}, bf16[192,2048]{1,0:T(8,128)(2,1)S(1)}, u32[]{:S(2)}, u32[]{:S(2)}) %collective-permute-start.29) | collective-permute-done | bytes 786464 | tf_op jit(solution)/shard_map/ppermute | solution.py:107
  314.0 16.8 %fusion.176 = f32[1536,2048]{1,0:T(8,128)} fusion(bf16[1536,2048]{1,0:T(8,128)(2,1)S(1)} %copy-done.68, bf16[384,1536]{1,0:T(8,128)(2,1)S(1)} %collective-permute-done.22, bf16[384,1536]{1,0:T(8,128)(2,1)S(1)} %collective-permute-done.21, bf16[384,1536]{1,0:T(8,128)(2,1)S(1)} %collective-permute-done.20, bf16[384,1536]{1,0:T(8,128)(2,1)S(1)} %fusion.47), kind=kOutput, calls=%fused_computation.319 | convolution fusion | flops 9682550784 | bytes 23592960 | tf_op jit(solution)/shard_map/dot_general | solution.py:55
  330.8 15.0 %multiply_convert_fusion.1 = (bf16[1536,1024]{1,0:T(8,128)(2,1)S(1)}, bf16[1536,1024]{1,0:T(8,128)(2,1)}, bf16[1536,1024]{1,0:T(8,128)(2,1)}) fusion(f32[1536,2048]{1,0:T(8,128)} %fusion.176, bf16[1536,1024]{1,0:T(8,128)(2,1)} %constant_dynamic-update-slice_fusion.31, bf16[384,1536]{1,0:T(8,128)(2,1)} %copy-done.42, bf16[384,1536]{1,0:T(8,128)(2,1)} %copy-done.41, ...), kind=kOutput, calls=%fused_computation.19 | convolution fusion | flops 4875878400 | bytes 29884416 | tf_op jit(solution)/shard_map/dot_general | solution.py:55
  345.8 6.8 fusion.92
  359.8 15.1 %convolution_convert_fusion.1 = bf16[1536,1536]{1,0:T(8,128)(2,1)} fusion(bf16[1536,2048]{1,0:T(8,128)(2,1)} %constant_dynamic-update-slice_fusion.22, bf16[1536,1024]{1,0:T(8,128)(2,1)} %get-tuple-element.19, bf16[1536,1024]{1,0:T(8,128)(2,1)S(1)} %get-tuple-element.18), kind=kOutput, calls=%fused_computation.14 | convolution fusion | flops 9678618624 | bytes 17301504 | tf_op jit(solution)/shard_map/dot_general | solution.py:65
  379.3 7.4 convolution_convert_fusion
  396.0 28.0 %collective-permute-done.59 = bf16[768,1024]{1,0:T(8,128)(2,1)} collective-permute-done((bf16[768,1024]{1,0:T(8,128)(2,1)}, bf16[768,1024]{1,0:T(8,128)(2,1)}, u32[]{:S(2)}, u32[]{:S(2)}) %collective-permute-start.59) | collective-permute-done | bytes 1572896 | tf_op jit(solution)/shard_map/ppermute | solution.py:107
  429.7 24.8 %collective-permute-done.56 = bf16[768,1024]{1,0:T(8,128)(2,1)S(1)} collective-permute-done((bf16[768,1024]{1,0:T(8,128)(2,1)}, bf16[768,1024]{1,0:T(8,128)(2,1)S(1)}, u32[]{:S(2)}, u32[]{:S(2)}) %collective-permute-start.56) | collective-permute-done | bytes 1572896 | tf_op jit(solution)/shard_map/ppermute | solution.py:107
  463.5 22.9 %collective-permute-done.57 = bf16[384,1024]{1,0:T(8,128)(2,1)S(1)} collective-permute-done((bf16[384,1024]{1,0:T(8,128)(2,1)S(1)}, bf16[384,1024]{1,0:T(8,128)(2,1)S(1)}, u32[]{:S(2)}, u32[]{:S(2)}) %collective-permute-start.57) | collective-permute-done | bytes 786464 | tf_op jit(solution)/shard_map/ppermute | solution.py:107
  496.8 9.9 %collective-permute-done.61 = bf16[192,1024]{1,0:T(8,128)(2,1)S(1)} collective-permute-done((bf16[192,1024]{1,0:T(8,128)(2,1)S(1)}, bf16[192,1024]{1,0:T(8,128)(2,1)S(1)}, u32[]{:S(2)}, u32[]{:S(2)}) %collective-permute-start.61) | collective-permute-done | bytes 393248 | tf_op jit(solution)/shard_map/ppermute | solution.py:107
  512.9 29.6 %psum.7 = f32[192]{0:T(256)} all-reduce(f32[192]{0:T(256)} %get-tuple-element.11), channel_id=1, replica_groups=mesh['dp'=8,'tensor'=4] {'tensor'}, use_global_device_ids=true, to_apply=%region_12.13 | all-reduce | flops 192 | bytes 1536 | tf_op jit(solution)/shard_map/psum | solution.py:311
  649.9 69.7 %collective-permute-done.52 = bf16[384,1536]{1,0:T(8,128)(2,1)S(1)} collective-permute-done((bf16[384,1536]{1,0:T(8,128)(2,1)S(1)}, bf16[384,1536]{1,0:T(8,128)(2,1)S(1)}, u32[]{:S(2)}, u32[]{:S(2)}) %collective-permute-start.52) | collective-permute-done | bytes 1179680 | tf_op jit(solution)/shard_map/ppermute | solution.py:107
  739.2 27.2 %collective-permute-done.47 = bf16[192,3072]{1,0:T(8,128)(2,1)S(1)} collective-permute-done((bf16[192,3072]{1,0:T(8,128)(2,1)S(1)}, bf16[192,3072]{1,0:T(8,128)(2,1)S(1)}, u32[]{:S(2)}, u32[]{:S(2)}) %collective-permute-start.47) | collective-permute-done | bytes 1179680 | tf_op jit(solution)/shard_map/ppermute | solution.py:107
  773.4 20.7 %collective-permute-done.48 = bf16[96,3072]{1,0:T(8,128)(2,1)S(1)} collective-permute-done((bf16[96,3072]{1,0:T(8,128)(2,1)S(1)}, bf16[96,3072]{1,0:T(8,128)(2,1)S(1)}, u32[]{:S(2)}, u32[]{:S(2)}) %collective-permute-start.48) | collective-permute-done | bytes 589856 | tf_op jit(solution)/shard_map/ppermute | solution.py:107
  796.6 6.7 collective-permute-done.49
  (471 shorter events, 359.3 us)
Async XLA Ops:
  0.7 112.3 %collective-permute-start.30 = (bf16[192,1024]{1,0:T(8,128)(2,1)}, bf16[192,1024]{1,0:T(8,128)(2,1)}, u32[]{:S(2)}, u32[]{:S(2)}) collective-permute-start(bf16[192,1024]{1,0:T(8,128)(2,1)} %bitcast.152), channel_id=1, source_target_pairs={{0,16},{1,17},{2,18},{3,19},{4,20},{5,21},{6,22},{7,23},{8,24},{9,... | collective-permute-start | bytes 1179656 | tf_op jit(solution)/shard_map/ppermute | solution.py:107
  4.8 109.7 %collective-permute-start.31 = (bf16[192,1024]{1,0:T(8,128)(2,1)}, bf16[192,1024]{1,0:T(8,128)(2,1)}, u32[]{:S(2)}, u32[]{:S(2)}) collective-permute-start(bf16[192,1024]{1,0:T(8,128)(2,1)} %bitcast.153), channel_id=1, source_target_pairs={{0,8},{1,9},{2,10},{3,11},{4,12},{5,13},{6,14},{7,15},{8,0},{9,1},... | collective-permute-start | bytes 1179656 | tf_op jit(solution)/shard_map/ppermute | solution.py:107
  26.1 90.0 %collective-permute-start.11 = (bf16[96,1536]{1,0:T(8,128)(2,1)}, bf16[96,1536]{1,0:T(8,128)(2,1)S(1)}, u32[]{:S(2)}, u32[]{:S(2)}) collective-permute-start(bf16[96,1536]{1,0:T(8,128)(2,1)} %get-tuple-element.42), channel_id=1, source_target_pairs={{0,16},{1,17},{2,18},{3,19},{4,20},{5,21},{6,22},{7,23},{8,24},{9,... | collective-permute-start | bytes 884744 | tf_op jit(solution)/shard_map/ppermute | solution.py:107
  112.1 65.9 %collective-permute-start.8 = (bf16[384,3200]{1,0:T(8,128)(2,1)}, bf16[384,3200]{1,0:T(8,128)(2,1)}, u32[]{:S(2)}, u32[]{:S(2)}) collective-permute-start(bf16[384,3200]{1,0:T(8,128)(2,1)} %constant_dynamic-update-slice_fusion), channel_id=1, source_target_pairs={{0,1},{1,0},{2,3},{3,2},{4,5},{5,4},{6,7},{7,6},{8,9},{9,8},{10,11... | collective-permute-start | bytes 7372808 | tf_op jit(solution)/shard_map/ppermute | solution.py:107
  112.9 66.1 %collective-permute-start.9 = (bf16[384,3200]{1,0:T(8,128)(2,1)}, bf16[384,3200]{1,0:T(8,128)(2,1)}, u32[]{:S(2)}, u32[]{:S(2)}) collective-permute-start(bf16[384,3200]{1,0:T(8,128)(2,1)} %constant_dynamic-update-slice_fusion.5), channel_id=1, source_target_pairs={{0,1},{1,0},{2,3},{3,2},{4,5},{5,4},{6,7},{7,6},{8,9},{9,8},{10,11... | collective-permute-start | bytes 7372808 | tf_op jit(solution)/shard_map/ppermute | solution.py:107
  141.3 104.0 %collective-permute-start.24 = (bf16[192,2048]{1,0:T(8,128)(2,1)}, bf16[192,2048]{1,0:T(8,128)(2,1)}, u32[]{:S(2)}, u32[]{:S(2)}) collective-permute-start(bf16[192,2048]{1,0:T(8,128)(2,1)} %get-tuple-element.35), channel_id=1, source_target_pairs={{0,8},{1,9},{2,10},{3,11},{4,12},{5,13},{6,14},{7,15},{8,0},{9,1},... | collective-permute-start | bytes 2359304 | tf_op jit(solution)/shard_map/ppermute | solution.py:107
  172.3 74.5 %collective-permute-start.26 = (bf16[192,2048]{1,0:T(8,128)(2,1)}, bf16[192,2048]{1,0:T(8,128)(2,1)}, u32[]{:S(2)}, u32[]{:S(2)}) collective-permute-start(bf16[192,2048]{1,0:T(8,128)(2,1)} %get-tuple-element.35), channel_id=1, source_target_pairs={{0,4},{1,5},{2,6},{3,7},{4,0},{5,1},{6,2},{7,3},{8,12},{9,13},{10,... | collective-permute-start | bytes 2359304 | tf_op jit(solution)/shard_map/ppermute | solution.py:107
  174.7 100.4 %collective-permute-start.39 = (bf16[384,1536]{1,0:T(8,128)(2,1)}, bf16[384,1536]{1,0:T(8,128)(2,1)}, u32[]{:S(2)}, u32[]{:S(2)}) collective-permute-start(bf16[384,1536]{1,0:T(8,128)(2,1)} %fusion.57), channel_id=1, source_target_pairs={{0,2},{1,3},{2,0},{3,1},{4,6},{5,7},{6,4},{7,5},{8,10},{9,11},{10,... | collective-permute-start | bytes 3538952 | tf_op jit(solution)/shard_map/ppermute | solution.py:107
  178.0 58.2 %collective-permute-start.18 = (bf16[384,1536]{1,0:T(8,128)(2,1)}, bf16[384,1536]{1,0:T(8,128)(2,1)}, u32[]{:S(2)}, u32[]{:S(2)}) collective-permute-start(bf16[384,1536]{1,0:T(8,128)(2,1)} %constant_dynamic-update-slice_fusion.11), channel_id=1, source_target_pairs={{0,1},{1,0},{2,3},{3,2},{4,5},{5,4},{6,7},{7,6},{8,9},{9,8},{10,11... | collective-permute-start | bytes 3538952 | tf_op jit(solution)/shard_map/ppermute | solution.py:107
  179.1 59.8 %collective-permute-start.19 = (bf16[384,1536]{1,0:T(8,128)(2,1)}, bf16[384,1536]{1,0:T(8,128)(2,1)}, u32[]{:S(2)}, u32[]{:S(2)}) collective-permute-start(bf16[384,1536]{1,0:T(8,128)(2,1)} %constant_dynamic-update-slice_fusion.16), channel_id=1, source_target_pairs={{0,1},{1,0},{2,3},{3,2},{4,5},{5,4},{6,7},{7,6},{8,9},{9,8},{10,11... | collective-permute-start | bytes 3538952 | tf_op jit(solution)/shard_map/ppermute | solution.py:107
  249.6 44.0 %collective-permute-start.20 = (bf16[384,1536]{1,0:T(8,128)(2,1)S(1)}, bf16[384,1536]{1,0:T(8,128)(2,1)S(1)}, u32[]{:S(2)}, u32[]{:S(2)}) collective-permute-start(bf16[384,1536]{1,0:T(8,128)(2,1)S(1)} %fusion.47), channel_id=1, source_target_pairs={{0,2},{1,3},{2,0},{3,1},{4,6},{5,7},{6,4},{7,5},{8,10},{9,11},{10,... | collective-permute-start | bytes 3538952 | tf_op jit(solution)/shard_map/ppermute | solution.py:107
  358.3 65.7 %collective-permute-start.59 = (bf16[768,1024]{1,0:T(8,128)(2,1)}, bf16[768,1024]{1,0:T(8,128)(2,1)}, u32[]{:S(2)}, u32[]{:S(2)}) collective-permute-start(bf16[768,1024]{1,0:T(8,128)(2,1)} %fusion.89), channel_id=1, source_target_pairs={{0,4},{1,5},{2,6},{3,7},{4,0},{5,1},{6,2},{7,3},{8,12},{9,13},{10,... | collective-permute-start | bytes 4718600 | tf_op jit(solution)/shard_map/ppermute | solution.py:107
  378.7 75.8 %collective-permute-start.56 = (bf16[768,1024]{1,0:T(8,128)(2,1)}, bf16[768,1024]{1,0:T(8,128)(2,1)S(1)}, u32[]{:S(2)}, u32[]{:S(2)}) collective-permute-start(bf16[768,1024]{1,0:T(8,128)(2,1)} %fusion.86), channel_id=1, source_target_pairs={{0,4},{1,5},{2,6},{3,7},{4,0},{5,1},{6,2},{7,3},{8,12},{9,13},{10,... | collective-permute-start | bytes 4718600 | tf_op jit(solution)/shard_map/ppermute | solution.py:107
  386.8 100.3 %collective-permute-start.42 = (bf16[768,1536]{1,0:T(8,128)(2,1)S(1)}, bf16[768,1536]{1,0:T(8,128)(2,1)}, u32[]{:S(2)}, u32[]{:S(2)}) collective-permute-start(bf16[768,1536]{1,0:T(8,128)(2,1)S(1)} %slice.327), channel_id=1, source_target_pairs={{0,1},{1,0},{2,3},{3,2},{4,5},{5,4},{6,7},{7,6},{8,9},{9,8},{10,11... | collective-permute-start | bytes 7077896 | tf_op jit(solution)/shard_map/ppermute | solution.py:107
  387.1 104.6 %collective-permute-start.37 = (bf16[768,1536]{1,0:T(8,128)(2,1)S(1)}, bf16[768,1536]{1,0:T(8,128)(2,1)}, u32[]{:S(2)}, u32[]{:S(2)}) collective-permute-start(bf16[768,1536]{1,0:T(8,128)(2,1)S(1)} %slice.323), channel_id=1, source_target_pairs={{0,1},{1,0},{2,3},{3,2},{4,5},{5,4},{6,7},{7,6},{8,9},{9,8},{10,11... | collective-permute-start | bytes 7077896 | tf_op jit(solution)/shard_map/ppermute | solution.py:107
  394.6 64.4 %collective-permute-start.63 = (bf16[384,1024]{1,0:T(8,128)(2,1)S(1)}, bf16[384,1024]{1,0:T(8,128)(2,1)S(1)}, u32[]{:S(2)}, u32[]{:S(2)}) collective-permute-start(bf16[384,1024]{1,0:T(8,128)(2,1)S(1)} %slice.497), channel_id=1, source_target_pairs={{0,8},{1,9},{2,10},{3,11},{4,12},{5,13},{6,14},{7,15},{8,0},{9,1},... | collective-permute-start | bytes 2359304 | tf_op jit(solution)/shard_map/ppermute | solution.py:107
  460.2 83.6 %collective-permute-start.64 = (bf16[192,1024]{1,0:T(8,128)(2,1)}, bf16[192,1024]{1,0:T(8,128)(2,1)}, u32[]{:S(2)}, u32[]{:S(2)}) collective-permute-start(bf16[192,1024]{1,0:T(8,128)(2,1)} %slice.503), channel_id=1, source_target_pairs={{0,16},{1,17},{2,18},{3,19},{4,20},{5,21},{6,22},{7,23},{8,24},{9,... | collective-permute-start | bytes 1179656 | tf_op jit(solution)/shard_map/ppermute | solution.py:107
  460.9 45.7 %collective-permute-start.61 = (bf16[192,1024]{1,0:T(8,128)(2,1)S(1)}, bf16[192,1024]{1,0:T(8,128)(2,1)S(1)}, u32[]{:S(2)}, u32[]{:S(2)}) collective-permute-start(bf16[192,1024]{1,0:T(8,128)(2,1)S(1)} %slice.504), channel_id=1, source_target_pairs={{0,16},{1,17},{2,18},{3,19},{4,20},{5,21},{6,22},{7,23},{8,24},{9,... | collective-permute-start | bytes 1179656 | tf_op jit(solution)/shard_map/ppermute | solution.py:107
  489.6 56.4 %collective-permute-start.43 = (bf16[384,1536]{1,0:T(8,128)(2,1)S(1)}, bf16[384,1536]{1,0:T(8,128)(2,1)}, u32[]{:S(2)}, u32[]{:S(2)}) collective-permute-start(bf16[384,1536]{1,0:T(8,128)(2,1)S(1)} %slice.495), channel_id=1, source_target_pairs={{0,2},{1,3},{2,0},{3,1},{4,6},{5,7},{6,4},{7,5},{8,10},{9,11},{10,... | collective-permute-start | bytes 3538952 | tf_op jit(solution)/shard_map/ppermute | solution.py:107
  495.3 272.0 %collective-permute-start.38 = (bf16[384,1536]{1,0:T(8,128)(2,1)}, bf16[384,1536]{1,0:T(8,128)(2,1)}, u32[]{:S(2)}, u32[]{:S(2)}) collective-permute-start(bf16[384,1536]{1,0:T(8,128)(2,1)} %slice.496), channel_id=1, source_target_pairs={{0,2},{1,3},{2,0},{3,1},{4,6},{5,7},{6,4},{7,5},{8,10},{9,11},{10,... | collective-permute-start | bytes 3538952 | tf_op jit(solution)/shard_map/ppermute | solution.py:107
  625.9 95.8 %collective-permute-start.44 = (bf16[384,3072]{1,0:T(8,128)(2,1)S(1)}, bf16[384,3072]{1,0:T(8,128)(2,1)S(1)}, u32[]{:S(2)}, u32[]{:S(2)}) collective-permute-start(bf16[384,3072]{1,0:T(8,128)(2,1)S(1)} %convolution_convert_fusion.3), channel_id=1, source_target_pairs={{0,1},{1,0},{2,3},{3,2},{4,5},{5,4},{6,7},{7,6},{8,9},{9,8},{10,11... | collective-permute-start | bytes 7077896 | tf_op jit(solution)/shard_map/ppermute | solution.py:107
  640.7 80.9 %collective-permute-start.46 = (bf16[384,3072]{1,0:T(8,128)(2,1)S(1)}, bf16[384,3072]{1,0:T(8,128)(2,1)S(1)}, u32[]{:S(2)}, u32[]{:S(2)}) collective-permute-start(bf16[384,3072]{1,0:T(8,128)(2,1)S(1)} %add_convert_fusion), channel_id=1, source_target_pairs={{0,2},{1,3},{2,0},{3,1},{4,6},{5,7},{6,4},{7,5},{8,10},{9,11},{10,... | collective-permute-start | bytes 7077896 | tf_op jit(solution)/shard_map/ppermute | solution.py:107
  642.5 77.0 %collective-permute-start.52 = (bf16[384,1536]{1,0:T(8,128)(2,1)S(1)}, bf16[384,1536]{1,0:T(8,128)(2,1)S(1)}, u32[]{:S(2)}, u32[]{:S(2)}) collective-permute-start(bf16[384,1536]{1,0:T(8,128)(2,1)S(1)} %add_convert_fusion.3), channel_id=1, source_target_pairs={{0,2},{1,3},{2,0},{3,1},{4,6},{5,7},{6,4},{7,5},{8,10},{9,11},{10,... | collective-permute-start | bytes 3538952 | tf_op jit(solution)/shard_map/ppermute | solution.py:107
  723.0 43.4 %collective-permute-start.47 = (bf16[192,3072]{1,0:T(8,128)(2,1)S(1)}, bf16[192,3072]{1,0:T(8,128)(2,1)S(1)}, u32[]{:S(2)}, u32[]{:S(2)}) collective-permute-start(bf16[192,3072]{1,0:T(8,128)(2,1)S(1)} %slice.494), channel_id=1, source_target_pairs={{0,8},{1,9},{2,10},{3,11},{4,12},{5,13},{6,14},{7,15},{8,0},{9,1},... | collective-permute-start | bytes 3538952 | tf_op jit(solution)/shard_map/ppermute | solution.py:107
  (124 other events, 2425.2 us)
where the time goes:
time: 816 us; the launch traced here: 806 us
  waiting for transfers between devices  386 us (47%)
  matrix products  181 us (22%)
  local copies, waits for them, and re-layouts  104 us (13%)
  starting transfers between devices  59.2 us (7%)
  other arithmetic  43.3 us (5%)
  blocking collectives  29.6 us (4%)
    ppermute x65, waiting for transfers between devices, swap(): return lax.ppermute(array, AXES, [(i, i ^ mask) for i in range(world)])  386 us
    dot_general x16, matrix products, against(): lax.dot_general(left_side, right_side, (((1,), (1,)), ((), ())), preferre...  67.4 us
    dot_general x14, matrix products, product(): return jnp.dot(left_side, right_side, preferred_element_type=f32)  66.6 us
    ppermute x65, starting transfers between devices, swap(): return lax.ppermute(array, AXES, [(i, i ^ mask) for i in range(world)])  59.2 us
    unnamed x201, local copies, waits for them, and re-layouts  42.8 us
    dot_general x14, matrix products, across(): lax.dot_general(left_side, right_side, (((0,), (0,)), ((), ())), preferre...  36.2 us
    psum x1, blocking collectives, per_device(): second = lax.psum(second, 'tensor')  29.6 us
  transfers between devices with their start and end apart: 65, of which 26 were waited for; matrix products, arithmetic and copies ran while one was open for 35% of the time, Pallas kernels for 0%

commit v1 on v0

--- a/solution.py
+++ b/solution.py
@@ -308,7 +308,9 @@
         second = jnp.sum(
             gate_weight.astype(f32) * gate_grad + up_weight.astype(f32) * up_grad, axis=1
         )
-        second = lax.psum(second, "tensor")
+        second = second
+        for hop in (1, 2):
+            second = second + lax.ppermute(second, "tensor", [(dev, dev ^ hop) for dev in range(4)])
         second = lax.dynamic_slice(second, (t_i * shard,), (shard,))
         second_gain_grad = second / second_gain.astype(f32)
         return (

time: 816 us -> 814 us (level)
  waiting for transfers between devices: 386 us -> 419 us
  blocking collectives: 29.6 us -> 0 us
    psum x1 -> x0, blocking collectives: 29.6 us -> none  [per_device(): second = lax.psum(second, 'tensor')]
    ppermute x0 -> x2, waiting for transfers between devices: none -> 25.7 us  [per_device(): lax.ppermute(second, 'tensor', [(dev, dev ^ hop) for dev in range(4)])]
    unnamed x201 -> x197, local copies, waits for them, and re-layouts: 42.8 us -> 43.1 us
  transfers between devices with their start and end apart: 65 -> 67, of which waited for: 26 -> 27; matrix products, arithmetic and copies ran while one was open for 35% -> 34% of each run, Pallas kernels for 0% -> 0%
where the time goes in v1:
time: 814 us; the launch traced here: 803 us
  waiting for transfers between devices  419 us (51%)
  matrix products  179 us (22%)
  local copies, waits for them, and re-layouts  104 us (13%)
  starting transfers between devices  57 us (7%)
  other arithmetic  40.7 us (5%)
    ppermute x65, waiting for transfers between devices, swap(): return lax.ppermute(array, AXES, [(i, i ^ mask) for i in range(world)])  393 us
    dot_general x14, matrix products, product(): return jnp.dot(left_side, right_side, preferred_element_type=f32)  66.6 us
    dot_general x16, matrix products, against(): lax.dot_general(left_side, right_side, (((1,), (1,)), ((), ())), preferre...  65.5 us
    ppermute x65, starting transfers between devices, swap(): return lax.ppermute(array, AXES, [(i, i ^ mask) for i in range(world)])  56.5 us
    unnamed x197, local copies, waits for them, and re-layouts  43.1 us
    dot_general x14, matrix products, across(): lax.dot_general(left_side, right_side, (((0,), (0,)), ((), ())), preferre...  36.2 us
    ppermute x2, waiting for transfers between devices, per_device(): lax.ppermute(second, 'tensor', [(dev, dev ^ hop) for dev in range(4)])  25.7 us
  transfers between devices with their start and end apart: 67, of which 27 were waited for; matrix products, arithmetic and copies ran while one was open for 34% of the time, Pallas kernels for 0%

profile of v1, /device:TPU:0, one launch (start us, length us, event | category | flops | bytes accessed | tf_op | source)
XLA Modules:
  0.0 803.2 jit_solution(9834053031612072950)
XLA Ops:
  29.8 8.6 %collective-permute-done.4 = bf16[96,3200]{1,0:T(8,128)(2,1)S(1)} collective-permute-done((bf16[96,3200]{1,0:T(8,128)(2,1)S(1)}, bf16[96,3200]{1,0:T(8,128)(2,1)S(1)}, u32[]{:S(2)}, u32[]{:S(2)}) %collective-permute-start.4) | collective-permute-done | bytes 614432 | tf_op jit(solution)/shard_map/ppermute | solution.py:107
  39.7 27.5 %collective-permute-done.1 = bf16[96,3200]{1,0:T(8,128)(2,1)S(1)} collective-permute-done((bf16[96,3200]{1,0:T(8,128)(2,1)S(1)}, bf16[96,3200]{1,0:T(8,128)(2,1)S(1)}, u32[]{:S(2)}, u32[]{:S(2)}) %collective-permute-start.1) | collective-permute-done | bytes 614432 | tf_op jit(solution)/shard_map/ppermute | solution.py:107
  76.1 8.4 %collective-permute-done.3 = bf16[96,3200]{1,0:T(8,128)(2,1)S(1)} collective-permute-done((bf16[96,3200]{1,0:T(8,128)(2,1)S(1)}, bf16[96,3200]{1,0:T(8,128)(2,1)S(1)}, u32[]{:S(2)}, u32[]{:S(2)}) %collective-permute-start.3) | collective-permute-done | bytes 614432 | tf_op jit(solution)/shard_map/ppermute | solution.py:107
  88.3 13.0 %collective-permute-done.6 = bf16[96,3200]{1,0:T(8,128)(2,1)S(1)} collective-permute-done((bf16[96,3200]{1,0:T(8,128)(2,1)S(1)}, bf16[96,3200]{1,0:T(8,128)(2,1)S(1)}, u32[]{:S(2)}, u32[]{:S(2)}) %collective-permute-start.6) | collective-permute-done | bytes 614432 | tf_op jit(solution)/shard_map/ppermute | solution.py:107
  102.2 9.9 %collective-permute-done.7 = bf16[96,3200]{1,0:T(8,128)(2,1)S(1)} collective-permute-done((bf16[96,3200]{1,0:T(8,128)(2,1)S(1)}, bf16[96,3200]{1,0:T(8,128)(2,1)S(1)}, u32[]{:S(2)}, u32[]{:S(2)}) %collective-permute-start.7) | collective-permute-done | bytes 614432 | tf_op jit(solution)/shard_map/ppermute | solution.py:107
  141.3 7.3 collective-permute-done.34
  149.2 23.1 %collective-permute-done.23 = bf16[192,2048]{1,0:T(8,128)(2,1)S(1)} collective-permute-done((bf16[192,2048]{1,0:T(8,128)(2,1)}, bf16[192,2048]{1,0:T(8,128)(2,1)S(1)}, u32[]{:S(2)}, u32[]{:S(2)}) %collective-permute-start.23) | collective-permute-done | bytes 786464 | tf_op jit(solution)/shard_map/ppermute | solution.py:107
  254.0 18.9 %collective-permute-done.36 = bf16[192,1024]{1,0:T(8,128)(2,1)S(1)} collective-permute-done((bf16[192,1024]{1,0:T(8,128)(2,1)S(1)}, bf16[192,1024]{1,0:T(8,128)(2,1)S(1)}, u32[]{:S(2)}, u32[]{:S(2)}) %collective-permute-start.36) | collective-permute-done | bytes 393248 | tf_op jit(solution)/shard_map/ppermute | solution.py:107
  280.1 13.4 %collective-permute-done.28 = bf16[192,2048]{1,0:T(8,128)(2,1)S(1)} collective-permute-done((bf16[192,2048]{1,0:T(8,128)(2,1)}, bf16[192,2048]{1,0:T(8,128)(2,1)S(1)}, u32[]{:S(2)}, u32[]{:S(2)}) %collective-permute-start.28) | collective-permute-done | bytes 786464 | tf_op jit(solution)/shard_map/ppermute | solution.py:107
  295.0 13.2 %collective-permute-done.29 = bf16[192,2048]{1,0:T(8,128)(2,1)S(1)} collective-permute-done((bf16[192,2048]{1,0:T(8,128)(2,1)S(1)}, bf16[192,2048]{1,0:T(8,128)(2,1)S(1)}, u32[]{:S(2)}, u32[]{:S(2)}) %collective-permute-start.29) | collective-permute-done | bytes 786464 | tf_op jit(solution)/shard_map/ppermute | solution.py:107
  314.0 16.8 %fusion.176 = f32[1536,2048]{1,0:T(8,128)} fusion(bf16[1536,2048]{1,0:T(8,128)(2,1)S(1)} %copy-done.66, bf16[384,1536]{1,0:T(8,128)(2,1)S(1)} %collective-permute-done.22, bf16[384,1536]{1,0:T(8,128)(2,1)S(1)} %collective-permute-done.21, bf16[384,1536]{1,0:T(8,128)(2,1)S(1)} %collective-permute-done.20, bf16[384,1536]{1,0:T(8,128)(2,1)S(1)} %fusion.47), kind=kOutput, calls=%fused_computation.319 | convolution fusion | flops 9682550784 | bytes 23592960 | tf_op jit(solution)/shard_map/dot_general | solution.py:55
  330.8 14.9 %multiply_convert_fusion.1 = (bf16[1536,1024]{1,0:T(8,128)(2,1)S(1)}, bf16[1536,1024]{1,0:T(8,128)(2,1)}, bf16[1536,1024]{1,0:T(8,128)(2,1)}) fusion(f32[1536,2048]{1,0:T(8,128)} %fusion.176, bf16[1536,1024]{1,0:T(8,128)(2,1)} %constant_dynamic-update-slice_fusion.31, bf16[384,1536]{1,0:T(8,128)(2,1)} %copy-done.40, bf16[384,1536]{1,0:T(8,128)(2,1)} %copy-done.39, ...), kind=kOutput, calls=%fused_computation.19 | convolution fusion | flops 4875878400 | bytes 29884416 | tf_op jit(solution)/shard_map/dot_general | solution.py:55
  345.8 6.8 fusion.92
  359.8 15.1 %convolution_convert_fusion.1 = bf16[1536,1536]{1,0:T(8,128)(2,1)} fusion(bf16[1536,2048]{1,0:T(8,128)(2,1)} %constant_dynamic-update-slice_fusion.22, bf16[1536,1024]{1,0:T(8,128)(2,1)} %get-tuple-element.19, bf16[1536,1024]{1,0:T(8,128)(2,1)S(1)} %get-tuple-element.18), kind=kOutput, calls=%fused_computation.14 | convolution fusion | flops 9678618624 | bytes 17301504 | tf_op jit(solution)/shard_map/dot_general | solution.py:65
  379.2 7.4 convolution_convert_fusion
  395.9 28.0 %collective-permute-done.59 = bf16[768,1024]{1,0:T(8,128)(2,1)} collective-permute-done((bf16[768,1024]{1,0:T(8,128)(2,1)}, bf16[768,1024]{1,0:T(8,128)(2,1)}, u32[]{:S(2)}, u32[]{:S(2)}) %collective-permute-start.59) | collective-permute-done | bytes 1572896 | tf_op jit(solution)/shard_map/ppermute | solution.py:107
  429.6 24.9 %collective-permute-done.56 = bf16[768,1024]{1,0:T(8,128)(2,1)S(1)} collective-permute-done((bf16[768,1024]{1,0:T(8,128)(2,1)}, bf16[768,1024]{1,0:T(8,128)(2,1)S(1)}, u32[]{:S(2)}, u32[]{:S(2)}) %collective-permute-start.56) | collective-permute-done | bytes 1572896 | tf_op jit(solution)/shard_map/ppermute | solution.py:107
  462.7 24.7 %collective-permute-done.57 = bf16[384,1024]{1,0:T(8,128)(2,1)S(1)} collective-permute-done((bf16[384,1024]{1,0:T(8,128)(2,1)S(1)}, bf16[384,1024]{1,0:T(8,128)(2,1)S(1)}, u32[]{:S(2)}, u32[]{:S(2)}) %collective-permute-start.57) | collective-permute-done | bytes 786464 | tf_op jit(solution)/shard_map/ppermute | solution.py:107
  492.1 12.7 %collective-permute-done.61 = bf16[192,1024]{1,0:T(8,128)(2,1)S(1)} collective-permute-done((bf16[192,1024]{1,0:T(8,128)(2,1)S(1)}, bf16[192,1024]{1,0:T(8,128)(2,1)S(1)}, u32[]{:S(2)}, u32[]{:S(2)}) %collective-permute-start.61) | collective-permute-done | bytes 393248 | tf_op jit(solution)/shard_map/ppermute | solution.py:107
  520.1 25.7 %collective-permute-done.63 = f32[192]{0:T(256)S(1)} collective-permute-done((f32[192]{0:T(256)S(1)}, f32[192]{0:T(256)S(1)}, u32[]{:S(2)}, u32[]{:S(2)}) %collective-permute-start.63) | collective-permute-done | bytes 800 | tf_op jit(solution)/shard_map/ppermute | solution.py:313
  648.3 69.7 %collective-permute-done.52 = bf16[384,1536]{1,0:T(8,128)(2,1)S(1)} collective-permute-done((bf16[384,1536]{1,0:T(8,128)(2,1)S(1)}, bf16[384,1536]{1,0:T(8,128)(2,1)S(1)}, u32[]{:S(2)}, u32[]{:S(2)}) %collective-permute-start.52) | collective-permute-done | bytes 1179680 | tf_op jit(solution)/shard_map/ppermute | solution.py:107
  735.0 29.8 %collective-permute-done.47 = bf16[192,3072]{1,0:T(8,128)(2,1)S(1)} collective-permute-done((bf16[192,3072]{1,0:T(8,128)(2,1)S(1)}, bf16[192,3072]{1,0:T(8,128)(2,1)S(1)}, u32[]{:S(2)}, u32[]{:S(2)}) %collective-permute-start.47) | collective-permute-done | bytes 1179680 | tf_op jit(solution)/shard_map/ppermute | solution.py:107
  771.5 20.1 %collective-permute-done.48 = bf16[96,3072]{1,0:T(8,128)(2,1)S(1)} collective-permute-done((bf16[96,3072]{1,0:T(8,128)(2,1)S(1)}, bf16[96,3072]{1,0:T(8,128)(2,1)S(1)}, u32[]{:S(2)}, u32[]{:S(2)}) %collective-permute-start.48) | collective-permute-done | bytes 589856 | tf_op jit(solution)/shard_map/ppermute | solution.py:107
  794.0 6.8 collective-permute-done.49
  (472 shorter events, 354.0 us)
Async XLA Ops:
  0.7 112.3 %collective-permute-start.30 = (bf16[192,1024]{1,0:T(8,128)(2,1)}, bf16[192,1024]{1,0:T(8,128)(2,1)}, u32[]{:S(2)}, u32[]{:S(2)}) collective-permute-start(bf16[192,1024]{1,0:T(8,128)(2,1)} %bitcast.152), channel_id=1, source_target_pairs={{0,16},{1,17},{2,18},{3,19},{4,20},{5,21},{6,22},{7,23},{8,24},{9,... | collective-permute-start | bytes 1179656 | tf_op jit(solution)/shard_map/ppermute | solution.py:107
  4.8 109.7 %collective-permute-start.31 = (bf16[192,1024]{1,0:T(8,128)(2,1)}, bf16[192,1024]{1,0:T(8,128)(2,1)}, u32[]{:S(2)}, u32[]{:S(2)}) collective-permute-start(bf16[192,1024]{1,0:T(8,128)(2,1)} %bitcast.153), channel_id=1, source_target_pairs={{0,8},{1,9},{2,10},{3,11},{4,12},{5,13},{6,14},{7,15},{8,0},{9,1},... | collective-permute-start | bytes 1179656 | tf_op jit(solution)/shard_map/ppermute | solution.py:107
  26.1 90.0 %collective-permute-start.11 = (bf16[96,1536]{1,0:T(8,128)(2,1)}, bf16[96,1536]{1,0:T(8,128)(2,1)S(1)}, u32[]{:S(2)}, u32[]{:S(2)}) collective-permute-start(bf16[96,1536]{1,0:T(8,128)(2,1)} %get-tuple-element.42), channel_id=1, source_target_pairs={{0,16},{1,17},{2,18},{3,19},{4,20},{5,21},{6,22},{7,23},{8,24},{9,... | collective-permute-start | bytes 884744 | tf_op jit(solution)/shard_map/ppermute | solution.py:107
  112.1 65.9 %collective-permute-start.8 = (bf16[384,3200]{1,0:T(8,128)(2,1)}, bf16[384,3200]{1,0:T(8,128)(2,1)}, u32[]{:S(2)}, u32[]{:S(2)}) collective-permute-start(bf16[384,3200]{1,0:T(8,128)(2,1)} %constant_dynamic-update-slice_fusion), channel_id=1, source_target_pairs={{0,1},{1,0},{2,3},{3,2},{4,5},{5,4},{6,7},{7,6},{8,9},{9,8},{10,11... | collective-permute-start | bytes 7372808 | tf_op jit(solution)/shard_map/ppermute | solution.py:107
  113.0 66.1 %collective-permute-start.9 = (bf16[384,3200]{1,0:T(8,128)(2,1)}, bf16[384,3200]{1,0:T(8,128)(2,1)}, u32[]{:S(2)}, u32[]{:S(2)}) collective-permute-start(bf16[384,3200]{1,0:T(8,128)(2,1)} %constant_dynamic-update-slice_fusion.5), channel_id=1, source_target_pairs={{0,1},{1,0},{2,3},{3,2},{4,5},{5,4},{6,7},{7,6},{8,9},{9,8},{10,11... | collective-permute-start | bytes 7372808 | tf_op jit(solution)/shard_map/ppermute | solution.py:107
  141.3 103.9 %collective-permute-start.24 = (bf16[192,2048]{1,0:T(8,128)(2,1)}, bf16[192,2048]{1,0:T(8,128)(2,1)}, u32[]{:S(2)}, u32[]{:S(2)}) collective-permute-start(bf16[192,2048]{1,0:T(8,128)(2,1)} %get-tuple-element.35), channel_id=1, source_target_pairs={{0,8},{1,9},{2,10},{3,11},{4,12},{5,13},{6,14},{7,15},{8,0},{9,1},... | collective-permute-start | bytes 2359304 | tf_op jit(solution)/shard_map/ppermute | solution.py:107
  172.3 74.5 %collective-permute-start.26 = (bf16[192,2048]{1,0:T(8,128)(2,1)}, bf16[192,2048]{1,0:T(8,128)(2,1)}, u32[]{:S(2)}, u32[]{:S(2)}) collective-permute-start(bf16[192,2048]{1,0:T(8,128)(2,1)} %get-tuple-element.35), channel_id=1, source_target_pairs={{0,4},{1,5},{2,6},{3,7},{4,0},{5,1},{6,2},{7,3},{8,12},{9,13},{10,... | collective-permute-start | bytes 2359304 | tf_op jit(solution)/shard_map/ppermute | solution.py:107
  174.7 100.4 %collective-permute-start.39 = (bf16[384,1536]{1,0:T(8,128)(2,1)}, bf16[384,1536]{1,0:T(8,128)(2,1)}, u32[]{:S(2)}, u32[]{:S(2)}) collective-permute-start(bf16[384,1536]{1,0:T(8,128)(2,1)} %fusion.57), channel_id=1, source_target_pairs={{0,2},{1,3},{2,0},{3,1},{4,6},{5,7},{6,4},{7,5},{8,10},{9,11},{10,... | collective-permute-start | bytes 3538952 | tf_op jit(solution)/shard_map/ppermute | solution.py:107
  178.0 58.2 %collective-permute-start.18 = (bf16[384,1536]{1,0:T(8,128)(2,1)}, bf16[384,1536]{1,0:T(8,128)(2,1)}, u32[]{:S(2)}, u32[]{:S(2)}) collective-permute-start(bf16[384,1536]{1,0:T(8,128)(2,1)} %constant_dynamic-update-slice_fusion.11), channel_id=1, source_target_pairs={{0,1},{1,0},{2,3},{3,2},{4,5},{5,4},{6,7},{7,6},{8,9},{9,8},{10,11... | collective-permute-start | bytes 3538952 | tf_op jit(solution)/shard_map/ppermute | solution.py:107
  179.1 59.7 %collective-permute-start.19 = (bf16[384,1536]{1,0:T(8,128)(2,1)}, bf16[384,1536]{1,0:T(8,128)(2,1)}, u32[]{:S(2)}, u32[]{:S(2)}) collective-permute-start(bf16[384,1536]{1,0:T(8,128)(2,1)} %constant_dynamic-update-slice_fusion.16), channel_id=1, source_target_pairs={{0,1},{1,0},{2,3},{3,2},{4,5},{5,4},{6,7},{7,6},{8,9},{9,8},{10,11... | collective-permute-start | bytes 3538952 | tf_op jit(solution)/shard_map/ppermute | solution.py:107
  249.5 44.0 %collective-permute-start.20 = (bf16[384,1536]{1,0:T(8,128)(2,1)S(1)}, bf16[384,1536]{1,0:T(8,128)(2,1)S(1)}, u32[]{:S(2)}, u32[]{:S(2)}) collective-permute-start(bf16[384,1536]{1,0:T(8,128)(2,1)S(1)} %fusion.47), channel_id=1, source_target_pairs={{0,2},{1,3},{2,0},{3,1},{4,6},{5,7},{6,4},{7,5},{8,10},{9,11},{10,... | collective-permute-start | bytes 3538952 | tf_op jit(solution)/shard_map/ppermute | solution.py:107
  358.3 65.7 %collective-permute-start.59 = (bf16[768,1024]{1,0:T(8,128)(2,1)}, bf16[768,1024]{1,0:T(8,128)(2,1)}, u32[]{:S(2)}, u32[]{:S(2)}) collective-permute-start(bf16[768,1024]{1,0:T(8,128)(2,1)} %fusion.89), channel_id=1, source_target_pairs={{0,4},{1,5},{2,6},{3,7},{4,0},{5,1},{6,2},{7,3},{8,12},{9,13},{10,... | collective-permute-start | bytes 4718600 | tf_op jit(solution)/shard_map/ppermute | solution.py:107
  378.6 75.8 %collective-permute-start.56 = (bf16[768,1024]{1,0:T(8,128)(2,1)}, bf16[768,1024]{1,0:T(8,128)(2,1)S(1)}, u32[]{:S(2)}, u32[]{:S(2)}) collective-permute-start(bf16[768,1024]{1,0:T(8,128)(2,1)} %fusion.86), channel_id=1, source_target_pairs={{0,4},{1,5},{2,6},{3,7},{4,0},{5,1},{6,2},{7,3},{8,12},{9,13},{10,... | collective-permute-start | bytes 4718600 | tf_op jit(solution)/shard_map/ppermute | solution.py:107
  386.8 101.2 %collective-permute-start.42 = (bf16[768,1536]{1,0:T(8,128)(2,1)S(1)}, bf16[768,1536]{1,0:T(8,128)(2,1)}, u32[]{:S(2)}, u32[]{:S(2)}) collective-permute-start(bf16[768,1536]{1,0:T(8,128)(2,1)S(1)} %slice.327), channel_id=1, source_target_pairs={{0,1},{1,0},{2,3},{3,2},{4,5},{5,4},{6,7},{7,6},{8,9},{9,8},{10,11... | collective-permute-start | bytes 7077896 | tf_op jit(solution)/shard_map/ppermute | solution.py:107
  388.5 122.9 %collective-permute-start.37 = (bf16[768,1536]{1,0:T(8,128)(2,1)}, bf16[768,1536]{1,0:T(8,128)(2,1)}, u32[]{:S(2)}, u32[]{:S(2)}) collective-permute-start(bf16[768,1536]{1,0:T(8,128)(2,1)} %slice.323), channel_id=1, source_target_pairs={{0,1},{1,0},{2,3},{3,2},{4,5},{5,4},{6,7},{7,6},{8,9},{9,8},{10,11... | collective-permute-start | bytes 7077896 | tf_op jit(solution)/shard_map/ppermute | solution.py:107
  394.5 64.5 %collective-permute-start.65 = (bf16[384,1024]{1,0:T(8,128)(2,1)S(1)}, bf16[384,1024]{1,0:T(8,128)(2,1)S(1)}, u32[]{:S(2)}, u32[]{:S(2)}) collective-permute-start(bf16[384,1024]{1,0:T(8,128)(2,1)S(1)} %slice.497), channel_id=1, source_target_pairs={{0,8},{1,9},{2,10},{3,11},{4,12},{5,13},{6,14},{7,15},{8,0},{9,1},... | collective-permute-start | bytes 2359304 | tf_op jit(solution)/shard_map/ppermute | solution.py:107
  459.4 59.7 %collective-permute-start.66 = (bf16[192,1024]{1,0:T(8,128)(2,1)S(1)}, bf16[192,1024]{1,0:T(8,128)(2,1)S(1)}, u32[]{:S(2)}, u32[]{:S(2)}) collective-permute-start(bf16[192,1024]{1,0:T(8,128)(2,1)S(1)} %slice.503), channel_id=1, source_target_pairs={{0,16},{1,17},{2,18},{3,19},{4,20},{5,21},{6,22},{7,23},{8,24},{9,... | collective-permute-start | bytes 1179656 | tf_op jit(solution)/shard_map/ppermute | solution.py:107
  459.7 45.0 %collective-permute-start.61 = (bf16[192,1024]{1,0:T(8,128)(2,1)S(1)}, bf16[192,1024]{1,0:T(8,128)(2,1)S(1)}, u32[]{:S(2)}, u32[]{:S(2)}) collective-permute-start(bf16[192,1024]{1,0:T(8,128)(2,1)S(1)} %slice.504), channel_id=1, source_target_pairs={{0,16},{1,17},{2,18},{3,19},{4,20},{5,21},{6,22},{7,23},{8,24},{9,... | collective-permute-start | bytes 1179656 | tf_op jit(solution)/shard_map/ppermute | solution.py:107
  490.5 55.9 %collective-permute-start.43 = (bf16[384,1536]{1,0:T(8,128)(2,1)S(1)}, bf16[384,1536]{1,0:T(8,128)(2,1)S(1)}, u32[]{:S(2)}, u32[]{:S(2)}) collective-permute-start(bf16[384,1536]{1,0:T(8,128)(2,1)S(1)} %slice.495), channel_id=1, source_target_pairs={{0,2},{1,3},{2,0},{3,1},{4,6},{5,7},{6,4},{7,5},{8,10},{9,11},{10,... | collective-permute-start | bytes 3538952 | tf_op jit(solution)/shard_map/ppermute | solution.py:107
  517.1 248.2 %collective-permute-start.38 = (bf16[384,1536]{1,0:T(8,128)(2,1)}, bf16[384,1536]{1,0:T(8,128)(2,1)}, u32[]{:S(2)}, u32[]{:S(2)}) collective-permute-start(bf16[384,1536]{1,0:T(8,128)(2,1)} %slice.496), channel_id=1, source_target_pairs={{0,2},{1,3},{2,0},{3,1},{4,6},{5,7},{6,4},{7,5},{8,10},{9,11},{10,... | collective-permute-start | bytes 3538952 | tf_op jit(solution)/shard_map/ppermute | solution.py:107
  624.3 94.2 %collective-permute-start.44 = (bf16[384,3072]{1,0:T(8,128)(2,1)S(1)}, bf16[384,3072]{1,0:T(8,128)(2,1)S(1)}, u32[]{:S(2)}, u32[]{:S(2)}) collective-permute-start(bf16[384,3072]{1,0:T(8,128)(2,1)S(1)} %convolution_convert_fusion.3), channel_id=1, source_target_pairs={{0,1},{1,0},{2,3},{3,2},{4,5},{5,4},{6,7},{7,6},{8,9},{9,8},{10,11... | collective-permute-start | bytes 7077896 | tf_op jit(solution)/shard_map/ppermute | solution.py:107
  639.1 79.4 %collective-permute-start.46 = (bf16[384,3072]{1,0:T(8,128)(2,1)S(1)}, bf16[384,3072]{1,0:T(8,128)(2,1)S(1)}, u32[]{:S(2)}, u32[]{:S(2)}) collective-permute-start(bf16[384,3072]{1,0:T(8,128)(2,1)S(1)} %add_convert_fusion), channel_id=1, source_target_pairs={{0,2},{1,3},{2,0},{3,1},{4,6},{5,7},{6,4},{7,5},{8,10},{9,11},{10,... | collective-permute-start | bytes 7077896 | tf_op jit(solution)/shard_map/ppermute | solution.py:107
  641.8 76.1 %collective-permute-start.52 = (bf16[384,1536]{1,0:T(8,128)(2,1)S(1)}, bf16[384,1536]{1,0:T(8,128)(2,1)S(1)}, u32[]{:S(2)}, u32[]{:S(2)}) collective-permute-start(bf16[384,1536]{1,0:T(8,128)(2,1)S(1)} %add_convert_fusion.3), channel_id=1, source_target_pairs={{0,2},{1,3},{2,0},{3,1},{4,6},{5,7},{6,4},{7,5},{8,10},{9,11},{10,... | collective-permute-start | bytes 3538952 | tf_op jit(solution)/shard_map/ppermute | solution.py:107
  719.9 44.9 %collective-permute-start.47 = (bf16[192,3072]{1,0:T(8,128)(2,1)S(1)}, bf16[192,3072]{1,0:T(8,128)(2,1)S(1)}, u32[]{:S(2)}, u32[]{:S(2)}) collective-permute-start(bf16[192,3072]{1,0:T(8,128)(2,1)S(1)} %slice.494), channel_id=1, source_target_pairs={{0,8},{1,9},{2,10},{3,11},{4,12},{5,13},{6,14},{7,15},{8,0},{9,1},... | collective-permute-start | bytes 3538952 | tf_op jit(solution)/shard_map/ppermute | solution.py:107
  (124 other events, 2466.6 us)
